TPU v7x, 32 devices: a whole 2x2x4 slice. The times are simulated.
32 devices in a mesh: row: 4 (over z), col: 8 (over y, x, core).
Axes of the slice: x: 2, y: 2, z: 4, core: 2. Of those that a mesh axis runs over, the one named last changes fastest.
Arguments:
- inverse_block: float32 [512, 512], P('row', 'col'), as said below
- panels: bfloat16 [2, 512, 512], P(None, 'row'), may hold values from -0.375 to 0.375
- pattern: int32 [2, 4], replicated, may hold values 0 or 1
Outputs:
- inverse_panel: float32 [2, 512, 512], P(None, ('row', 'col'))
- update: float32 [2, 512, 512], P(None, 'col')
Inputs may be any that keep to these rules, and one draw needn't show every extreme that they name: `pattern`: 1 marks a block of rows in the supernode's structure, 0 a block outside it. `inverse_block`: symmetric.
All inputs are finite; a program needn't handle non-finite values.
Results may differ from a plain program's by a relative error of at most 0.00045.
Values may be sent and summed in bfloat16 or wider, within the bound.
No kernel may reach another device: no remote copies, remote signals or barrier semaphores. Data moves between devices by JAX's collectives and lax.ppermute only.
A program may use at most 64 MiB of HBM per device.

v0:
```python
import jax
import jax.numpy as jnp
from jax import lax
from jax.sharding import PartitionSpec as P

BLOCK = 128


def spread(block, axis, source):
    block = jnp.where(lax.axis_index(axis) == source, block, jnp.zeros_like(block))
    return lax.psum(block, axis)


def shards(inverse_block, panels, pattern):
    row_count = lax.axis_size("row")
    col_count = lax.axis_size("col")
    row_index = lax.axis_index("row")
    col_index = lax.axis_index("col")
    rows_here = panels.shape[1]
    cols_here = inverse_block.shape[1]
    ratio = col_count // row_count
    span = rows_here // col_count
    width = panels.shape[2]
    blocks = pattern.shape[1]
    row_ids = row_index * rows_here + jnp.arange(rows_here, dtype=jnp.int32)
    onehot = (row_ids // BLOCK)[:, None] == jnp.arange(blocks, dtype=jnp.int32)[None, :]
    row_mask = jnp.sum(jnp.where(onehot[None, :, :], pattern[:, None, :], 0), axis=2)
    used = panels * row_mask[:, :, None].astype(jnp.bfloat16)
    piece = lax.dynamic_slice_in_dim(used, col_index % ratio * cols_here, cols_here, 1)
    col_panel = spread(piece, "row", col_index // ratio)
    product = jnp.einsum(
        "ij,sjw->siw", inverse_block, col_panel.astype(jnp.float32), precision=lax.Precision.HIGHEST
    )
    term = -(product * row_mask[:, :, None].astype(jnp.float32))
    share = width // col_count
    partial_update = jnp.einsum(
        "siv,siw->svw", used.astype(jnp.float32), term, precision=lax.Precision.HIGHEST
    )
    panel_parts = term.reshape(2, col_count, span, width)
    update_parts = partial_update.reshape(2, col_count, share, width)
    joined = jnp.concatenate([panel_parts, update_parts], axis=2).reshape(
        2, col_count * (span + share), width
    )
    received = lax.psum_scatter(joined, "col", scatter_dimension=1, tiled=True)
    inverse_panel = received[:, :span]
    update = -lax.psum(received[:, span:], "row")
    return (inverse_panel, update)


def solution(mesh):
    return jax.shard_map(
        shards,
        mesh=mesh,
        in_specs=(P("row", "col"), P(None, "row", None), P()),
        out_specs=(P(None, ("row", "col"), None), P(None, "col", None)),
        check_vma=False,
    )
```

profile of v0, /device:TPU:0, one launch (start us, length us, event | category | flops | bytes accessed | tf_op | source)
XLA Modules:
  0.0 142.5 jit_solution(808378041422368606)
XLA Ops:
  7.2 0.0 copy-start
  7.2 0.0 all-reduce.3.cloned.1.call-start
  7.3 0.8 select_reduce_fusion
  8.1 1.1 broadcast_multiply_fusion
  9.1 0.7 dynamic-slice_select_fusion
  9.8 0.0 all-reduce.3.cloned.1.call-update
  9.8 0.0 reduce-scatter.2.cloned.1.call-start
  9.9 38.4 %all-reduce.3.cloned.1.call-done = bf16[2,64,512]{2,1,0:T(8,128)(2,1)} async-done(((bf16[2,64,512]{2,1,0:T(8,128)(2,1)}), bf16[2,64,512]{2,1,0:T(8,128)(2,1)}) %all-reduce.3.cloned.1.call-update) | async-done | bytes 131088 | tf_op jit(solution)/shard_map/psum | solution.py:11
  48.3 0.0 copy-done
  48.3 1.3 fusion
  49.6 1.0 fusion.3
  50.7 1.7 %pad_maximum_fusion = f32[2,8,80,512]{3,2,1,0:T(8,128)} fusion(f32[2,8,64,512]{3,2,1,0:T(8,128)S(1)} %bitcast.12, f32[2,8,16,512]{3,2,1,0:T(8,128)S(1)} %bitcast.13), kind=kLoop, calls=%fused_computation | loop fusion | flops 655360 | bytes 5242880 | tf_op jit(solution)/shard_map/concatenate | solution.py:41
  52.4 0.0 reduce-scatter.2.cloned.1.call-update
  52.4 0.0 all-reduce.5.cloned.1.call-start
  52.5 43.3 %reduce-scatter.2.cloned.1.call-done = f32[2,80,512]{2,1,0:T(8,128)} async-done(((f32[2,640,512]{2,1,0:T(8,128)}), f32[2,80,512]{2,1,0:T(8,128)}) %reduce-scatter.2.cloned.1.call-update) | async-done | bytes 327696 | tf_op jit(solution)/shard_map/reduce_scatter | solution.py:44
  95.8 1.7 %slice.9 = f32[2,64,512]{2,1,0:T(8,128)} slice(f32[2,80,512]{2,1,0:T(8,128)} %reduce-scatter.2.cloned.1.call-done), slice={[0:2], [16:80], [0:512]} | slice | bytes 524288 | tf_op jit(solution)/shard_map/slice | solution.py:46
  97.4 0.0 all-reduce.5.cloned.1.call-update
  97.5 1.5 %slice.8 = f32[2,16,512]{2,1,0:T(8,128)} slice(f32[2,80,512]{2,1,0:T(8,128)} %reduce-scatter.2.cloned.1.call-done), slice={[0:2], [0:16], [0:512]} | slice | bytes 131072 | tf_op jit(solution)/shard_map/slice | solution.py:45
  98.9 35.4 %all-reduce.5.cloned.1.call-done = f32[2,64,512]{2,1,0:T(8,128)} async-done(((f32[2,64,512]{2,1,0:T(8,128)}), f32[2,64,512]{2,1,0:T(8,128)}) %all-reduce.5.cloned.1.call-update) | async-done | bytes 262160 | tf_op jit(solution)/shard_map/psum | solution.py:46
  134.3 1.7 %neg.11 = f32[2,64,512]{2,1,0:T(8,128)} negate(f32[2,64,512]{2,1,0:T(8,128)} %all-reduce.5.cloned.1.call-done) | non-fusion elementwise | flops 65536 | bytes 524288 | tf_op jit(solution)/shard_map/neg | solution.py:46
  (3 shorter events, 0.0 us)
Async XLA Ops:
  7.2 41.1 %copy-start = (f32[128,64]{0,1:T(8,128)S(1)}, f32[128,64]{0,1:T(8,128)}, u32[]{:S(2)}) copy-start(f32[128,64]{0,1:T(8,128)} %param.3) | copy-start | bytes 98308
  7.2 41.1 %all-reduce.3.cloned.1.call-start = ((), (), s32[]{:S(2)}) async-start(), calls=%async_computation.1 | async-start | bytes 262144 | tf_op jit(solution)/shard_map/psum | solution.py:11
  9.8 85.9 %reduce-scatter.2.cloned.1.call-start = ((), (), s32[]{:S(2)}) async-start(), calls=%async_computation.2 | async-start | bytes 2949120 | tf_op jit(solution)/shard_map/reduce_scatter | solution.py:44
  52.4 81.9 %all-reduce.5.cloned.1.call-start = ((), (), s32[]{:S(2)}) async-start(), calls=%async_computation.3 | async-start | bytes 524288 | tf_op jit(solution)/shard_map/psum | solution.py:46
Sparse Core Ops, SparseCore 0:
  10.9 37.3 all-reduce.2
  52.5 43.1 reduce-scatter.1
  98.7 35.5 all-reduce.4
where the time goes:
time: 143 us; the launch traced here: 142 us
  waiting for transfers between devices  117 us (82%)
  between operations  13.8 us (10%)
  other arithmetic  5.95 us (4%)
  local copies, waits for them, and re-layouts  3.16 us (2%)
  matrix products  2.35 us (2%)
    reduce_scatter x1, waiting for transfers between devices, shards(): received = lax.psum_scatter(joined, 'col', scatter_dimension=1, tiled=True)  43.3 us
    psum x1, waiting for transfers between devices, spread(): return lax.psum(block, axis)  38.4 us
    psum x1, waiting for transfers between devices, shards(): update = -lax.psum(received[:, span:], 'row')  35.4 us
  transfers between devices with their start and end apart: 3, of which 3 were waited for; matrix products, arithmetic and copies ran while one was open for 1% of the time, Pallas kernels for 0%

commit v1 on v0

--- a/solution.py
+++ b/solution.py
@@ -1,9 +1,17 @@
 import jax
 import jax.numpy as jnp
 from jax import lax
+from jax.experimental import pallas as pl
+from jax.experimental.pallas import tpu as pltpu
 from jax.sharding import PartitionSpec as P
 
-BLOCK = 128
+
+LANES = 128
+LOCAL_BYTES = 4 << 20
+KERNEL_VMEM = 16 << 20
+PACK_PARAMS = pltpu.CompilerParams(vmem_limit_bytes=KERNEL_VMEM)
+SECOND = {1: 3, 2: 1, 3: 2}
+SOURCE = {by ^ second: by for by, second in SECOND.items()}
 
 
 def spread(block, axis, source):
@@ -11,19 +19,20 @@
     return lax.psum(block, axis)
 
 
-def shards(inverse_block, panels, pattern):
+def reducing(inverse_block, panels, pattern):
     row_count = lax.axis_size("row")
     col_count = lax.axis_size("col")
     row_index = lax.axis_index("row")
     col_index = lax.axis_index("col")
     rows_here = panels.shape[1]
     cols_here = inverse_block.shape[1]
+    width = panels.shape[2]
+    blocks = pattern.shape[1]
+    block = rows_here * row_count // blocks
     ratio = col_count // row_count
     span = rows_here // col_count
-    width = panels.shape[2]
-    blocks = pattern.shape[1]
     row_ids = row_index * rows_here + jnp.arange(rows_here, dtype=jnp.int32)
-    onehot = (row_ids // BLOCK)[:, None] == jnp.arange(blocks, dtype=jnp.int32)[None, :]
+    onehot = (row_ids // block)[:, None] == jnp.arange(blocks, dtype=jnp.int32)[None, :]
     row_mask = jnp.sum(jnp.where(onehot[None, :, :], pattern[:, None, :], 0), axis=2)
     used = panels * row_mask[:, :, None].astype(jnp.bfloat16)
     piece = lax.dynamic_slice_in_dim(used, col_index % ratio * cols_here, cols_here, 1)
@@ -47,11 +56,279 @@
     return (inverse_panel, update)
 
 
+def halves(value):
+    high = value.astype(jnp.bfloat16)
+    return high, (value - high.astype(jnp.float32)).astype(jnp.bfloat16)
+
+
+def pack_kernel(a_hbm, panels_hbm, a_out, last_out, panel_out, a_in, panel_in, sems):
+    col = lax.axis_index("col")
+    a_copy = pltpu.make_async_copy(a_hbm, a_in, sems.at[0])
+    panel_copy = pltpu.make_async_copy(panels_hbm.at[col % 2], panel_in, sems.at[1])
+    a_copy.start()
+    panel_copy.start()
+    a_copy.wait()
+    packed = jnp.concatenate(halves(a_in[...]), axis=0)
+    a_out[...] = packed
+    last_out[0] = packed
+    panel_copy.wait()
+    for b in range(panel_out.shape[0]):
+        panel_out[b] = panel_in[:, b * LANES : (b + 1) * LANES]
+    last_out[1] = panel_in[:, pl.ds(pl.multiple_of(col // 2 * LANES, LANES), LANES)]
+
+
+def arrange_kernel(own, first, second, last, mine, *rest):
+    outs, turned = rest[:-1], rest[-1]
+    tile = own.shape[0]
+    row = lax.axis_index("row")
+    chip = lax.axis_index("col") // 2
+    chips = len(outs) + 1
+    few = tile // chips
+    mine[pl.ds(pl.multiple_of(row * tile, tile), tile), :] = own[...]
+    mine[pl.ds(pl.multiple_of((row ^ 1) * tile, tile), tile), :] = first[...]
+    mine[pl.ds(pl.multiple_of((row ^ 2) * tile, tile), tile), :] = second[...]
+    mine[pl.ds(pl.multiple_of((row ^ 3) * tile, tile), tile), :] = last[0]
+    mine[chips * tile : (chips + 1) * tile, :] = last[1]
+    turned[...] = own[...].astype(jnp.float32).T
+    here = pl.ds(pl.multiple_of(chip * few, few), few)
+    mine[(chips + 1) * tile :, :] = turned[here, :].astype(jnp.bfloat16)
+    for by, out in enumerate(outs, 1):
+        other = chip ^ SECOND[by]
+        out[:tile] = mine[pl.ds(pl.multiple_of(chip * tile, tile), tile), :]
+        out[tile : 2 * tile] = mine[pl.ds(pl.multiple_of(other * tile, tile), tile), :]
+        out[2 * tile : 3 * tile] = last[1]
+        there = pl.ds(pl.multiple_of((chip ^ by) * few, few), few)
+        out[3 * tile :] = turned[there, :].astype(jnp.bfloat16)
+
+
+def local_kernel(pattern_ref, panels_ref, *refs):
+    firsts, seconds = refs[:2], refs[2:4]
+    owns, others = refs[4:6], refs[6:12]
+    inverse_out, update_out, used, rhs, y, lhs = refs[12:]
+    row = lax.axis_index("row")
+    col = lax.axis_index("col")
+    core = col % 2
+    chip = col // 2
+    rows, width = panels_ref.shape[1:]
+    tile = rows
+    half = tile // 2
+    chips = width // tile
+    share = update_out.shape[1]
+    span = inverse_out.shape[1]
+    block = used.shape[1] // pattern_ref.shape[1]
+    sides = (core, 1 - core)
+
+    def at(index, size):
+        return pl.ds(pl.multiple_of(index * size, size), size)
+
+    def keep(s, owner, lanes, read):
+        for start in range(0, rows, block):
+            flag = pattern_ref[s, (owner * rows + start) // block]
+            value = read(pl.ds(start, block))
+            to = pl.ds(pl.multiple_of(owner * rows + start, block), block)
+            used[s, to, lanes] = jnp.where(flag != 0, value, jnp.zeros_like(value))
+
+    for s in range(2):
+        keep(s, row, slice(None), lambda r: panels_ref[s, r, :])
+    for side in range(2):
+        s = sides[side]
+        for b in range(chips):
+            lanes = pl.ds(b * LANES, LANES)
+            keep(s, row ^ 1, lanes, lambda r: firsts[side][b, r, :])
+            keep(s, row ^ 2, lanes, lambda r: seconds[side][b, r, :])
+        keep(s, row ^ 3, at(chip, LANES), lambda r: owns[side][pl.ds(chips * tile + r.start, block), :])
+        for by in range(1, chips):
+            other = others[2 * (by - 1) + side]
+            keep(s, row ^ 3, at(chip ^ by, LANES), lambda r: other[pl.ds(2 * tile + r.start, block), :])
+
+    mine = at(chip, LANES)
+    for s in range(2):
+        rhs[:, s * LANES : (s + 1) * LANES] = used[s, :, mine]
+
+    def dot(a, b):
+        return jnp.dot(a, b, preferred_element_type=jnp.float32)
+
+    def folded(which, side, value):
+        to = pl.ds(pl.multiple_of(which * tile + sides[side] * half, half), half)
+        start = side * tile
+        return to, value[start : start + half] + value[start + half : start + tile]
+
+    def twice(which):
+        pieces = []
+        for side in range(2):
+            piece = rhs[pl.ds(pl.multiple_of(which * tile + sides[side] * half, half), half), :]
+            pieces += [piece, piece]
+        return pieces
+
+    def turn(ref, start):
+        return ref[start, :].T
+
+    stack = jnp.concatenate(
+        [
+            jnp.concatenate([owns[side][i * tile : (i + 1) * tile, :] for i in range(chips)], axis=1)
+            for side in range(2)
+        ],
+        axis=0,
+    )
+    value = dot(stack, rhs[...])
+    for side in range(2):
+        to, part = folded(chip, side, value)
+        y[to, :] = part
+    own_twice = twice(chip)
+    for by in range(1, chips):
+        pair = others[2 * (by - 1) : 2 * by]
+        which = chip ^ by
+        source = SOURCE[by]
+        far = others[2 * (source - 1) : 2 * source]
+        turned = [turn(owns[side], at(which, tile)) for side in range(2)]
+        turned += [turn(far[side], pl.ds(tile, tile)) for side in range(2)]
+        y[at(which, tile), :] = dot(
+            jnp.concatenate(turned, axis=1),
+            jnp.concatenate(own_twice + twice(chip ^ source), axis=0),
+        )
+        stack = jnp.concatenate(
+            [
+                jnp.concatenate([pair[side][:tile, :], pair[side][tile : 2 * tile, :]], axis=1)
+                for side in range(2)
+            ],
+            axis=0,
+        )
+        value = dot(
+            stack,
+            jnp.concatenate([rhs[at(which, tile), :], rhs[at(which ^ SECOND[by], tile), :]], axis=0),
+        )
+        for side in range(2):
+            to, part = folded(which, side, value)
+            y[to, :] += part
+
+    for by in range(chips):
+        if by == 0:
+            pair, start = owns, (chips + 1) * tile
+        else:
+            pair, start = others[2 * (by - 1) : 2 * by], 3 * tile
+        a, b = [
+            pair[side][pl.ds(pl.multiple_of(start + core * span, span), span), :].astype(jnp.float32)
+            for side in range(2)
+        ]
+        a, b = jnp.where(core == 0, a, b), jnp.where(core == 0, b, a)
+        lanes = at(chip ^ by, LANES)
+        high = jnp.concatenate([a[:, :half], b[:, :half]], axis=1)
+        low = jnp.concatenate([a[:, half:], b[:, half:]], axis=1)
+        lhs[2 * share : 2 * share + span, lanes] = high.astype(jnp.bfloat16)
+        lhs[2 * share + span :, lanes] = low.astype(jnp.bfloat16)
+
+    for s in range(2):
+        y_t = y[:, s * LANES : (s + 1) * LANES].T
+        high, low = halves(jnp.where(core == 0, y_t[:share], y_t[share:]))
+        lhs[:share] = high
+        lhs[share : 2 * share] = low
+        out = dot(lhs[...], used[s])
+        update_out[s] = out[:share] + out[share : 2 * share]
+        flag = pattern_ref[s, (row * rows + col * span) // block]
+        product = out[2 * share : 2 * share + span] + out[2 * share + span :]
+        inverse_out[s] = jnp.where(flag != 0, -product, jnp.zeros_like(product))
+
+
+def gathering(inverse_block, panels, pattern):
+    return gathered(inverse_block, panels, pattern)
+
+
+def gathered(inverse_block, panels, pattern):
+    col_count = lax.axis_size("col")
+    _, rows, width = panels.shape
+    tile = rows
+    chips = col_count // 2
+    height = rows * lax.axis_size("row")
+    cols = inverse_block.shape[1]
+    share = width // col_count
+    span = rows // col_count
+    vmem = pl.BlockSpec(memory_space=pltpu.VMEM)
+    hbm = pl.BlockSpec(memory_space=pltpu.HBM)
+    params = pltpu.CompilerParams(vmem_limit_bytes=KERNEL_VMEM)
+
+    def bf16(*shape):
+        return jax.ShapeDtypeStruct(shape, jnp.bfloat16)
+
+    def swap(value, axis, by):
+        return lax.ppermute(value, axis, [(i, i ^ by) for i in range(lax.axis_size(axis))])
+
+    a, last, panel = pl.pallas_call(
+        pack_kernel,
+        out_shape=(bf16(tile, LANES), bf16(2, tile, LANES), bf16(chips, tile, LANES)),
+        in_specs=[hbm] * 2,
+        out_specs=(vmem,) * 3,
+        scratch_shapes=[
+            pltpu.VMEM((cols, rows), jnp.float32),
+            pltpu.VMEM((rows, width), jnp.bfloat16),
+            pltpu.SemaphoreType.DMA((2,)),
+        ],
+        compiler_params=PACK_PARAMS,
+    )(inverse_block.T, panels)
+    second_a = swap(a, "row", 2)
+    last = swap(last, "row", 3)
+    first_a = swap(a, "row", 1)
+    second = swap(panel, "row", 2)
+    first = swap(panel, "row", 1)
+    few = tile // chips
+    own, *sent = pl.pallas_call(
+        arrange_kernel,
+        out_shape=(bf16((chips + 1) * tile + few, LANES),) + (bf16(3 * tile + few, LANES),) * (chips - 1),
+        in_specs=[vmem] * 4,
+        out_specs=(vmem,) * chips,
+        scratch_shapes=[pltpu.VMEM((tile, LANES), jnp.float32)],
+        compiler_params=params,
+    )(a, first_a, second_a, last)
+    others = []
+    for by, value in enumerate(sent, 1):
+        value = swap(value, "col", 2 * by)
+        others += [value, swap(value, "col", 1)]
+    return pl.pallas_call(
+        local_kernel,
+        out_shape=(
+            jax.ShapeDtypeStruct((2, span, width), jnp.float32),
+            jax.ShapeDtypeStruct((2, share, width), jnp.float32),
+        ),
+        in_specs=[pl.BlockSpec(memory_space=pltpu.SMEM)] + [vmem] * (7 + 2 * (chips - 1)),
+        out_specs=(vmem,) * 2,
+        scratch_shapes=[
+            pltpu.VMEM((2, height, width), jnp.bfloat16),
+            pltpu.VMEM((height, 2 * LANES), jnp.bfloat16),
+            pltpu.VMEM((height, 2 * LANES), jnp.float32),
+            pltpu.VMEM((2 * share + 2 * span, height), jnp.bfloat16),
+        ],
+        compiler_params=params,
+    )(pattern, panels, first, swap(first, "col", 1), second, swap(second, "col", 1), own, swap(own, "col", 1), *others)
+
+
+def fits(mesh, inverse_block, panels, pattern):
+    row_count, col_count = mesh.shape["row"], mesh.shape["col"]
+    height, width = inverse_block.shape[0], panels.shape[2]
+    rows, cols = height // row_count, height // col_count
+    block = height // pattern.shape[1]
+    return (
+        row_count == len(SECOND) + 1
+        and col_count == 2 * row_count
+        and width == LANES * row_count
+        and inverse_block.size * 4 <= LOCAL_BYTES
+        and 2 * cols == LANES
+        and 2 * (width // col_count) == LANES
+        and rows == 2 * cols
+        and rows % block == 0
+        and block % 16 == 0
+        and (rows // col_count) % 16 == 0
+    )
+
+
 def solution(mesh):
-    return jax.shard_map(
-        shards,
-        mesh=mesh,
-        in_specs=(P("row", "col"), P(None, "row", None), P()),
-        out_specs=(P(None, ("row", "col"), None), P(None, "col", None)),
-        check_vma=False,
-    )
+    def run(inverse_block, panels, pattern):
+        body = gathering if fits(mesh, inverse_block, panels, pattern) else reducing
+        mapped = jax.shard_map(
+            body,
+            mesh=mesh,
+            in_specs=(P("row", "col"), P(None, "row", None), P()),
+            out_specs=(P(None, ("row", "col"), None), P(None, "col", None)),
+            check_vma=False,
+        )
+        return mapped(inverse_block, panels, pattern)
+
+    return run

time: 143 us -> 31.1 us (0.22)
  waiting for transfers between devices: 117 us -> 11.7 us
  starting transfers between devices: 0.12 us -> 13.9 us
  between operations: 13.8 us -> 0.68 us
  other arithmetic: 5.95 us -> 0 us
  Pallas kernels: 0 us -> 2.88 us
  matrix products: 2.35 us -> 0 us
  local copies, waits for them, and re-layouts: 3.16 us -> 1.71 us
    psum x2 -> x0, waiting for transfers between devices: 73.8 us -> none  [the longest x1 38.4 us: spread(): return lax.psum(block, axis)]
    reduce_scatter x1 -> x0, waiting for transfers between devices: 43.3 us -> none  [shards(): received = lax.psum_scatter(joined, 'col', scatter_dimension=1, tiled=True)]
    ppermute x0 -> x14, starting transfers between devices: none -> 13.9 us  [swap(): lax.ppermute(value, axis, [(i, i ^ by) for i in range(lax.axis_size(axis))])]
    ppermute x0 -> x14, waiting for transfers between devices: none -> 11.7 us  [swap(): lax.ppermute(value, axis, [(i, i ^ by) for i in range(lax.axis_size(axis))])]
    slice x2 -> x0, local copies, waits for them, and re-layouts: 3.15 us -> none  [the longest x1 1.67 us: shards(): update = -lax.psum(received[:, span:], 'row')]
    pallas_call x0 -> x3, Pallas kernels: none -> 2.88 us  [the longest x1 2.51 us: gathered(): pl.pallas_call(local_kernel, out_shape=(jax.ShapeDtypeStruct((2, span, wi...]
    dot_general x2 -> x0, matrix products: 2.35 us -> none  [the longest x1 1.32 us: shards(): jnp.einsum('ij,sjw->siw', inverse_block, col_panel.astype(jnp.float32), p...]
    concatenate x1 -> x0, other arithmetic: 1.74 us -> none  [shards(): jnp.concatenate([panel_parts, update_parts], axis=2)]
  transfers between devices with their start and end apart: 3 -> 14, of which waited for: 3 -> 6; matrix products, arithmetic and copies ran while one was open for 1% -> 0% of each run, Pallas kernels for 0% -> 0%
where the time goes in v1:
time: 31.1 us; the launch traced here: 30.9 us
  starting transfers between devices  13.9 us (45%)
  waiting for transfers between devices  11.7 us (38%)
  Pallas kernels  2.88 us (9%)
  local copies, waits for them, and re-layouts  1.71 us (5%)
  between operations  0.68 us (2%)
    ppermute x14, starting transfers between devices, swap(): lax.ppermute(value, axis, [(i, i ^ by) for i in range(lax.axis_size(axis))])  13.9 us
    ppermute x14, waiting for transfers between devices, swap(): lax.ppermute(value, axis, [(i, i ^ by) for i in range(lax.axis_size(axis))])  11.7 us
    pallas_call x1, Pallas kernels, gathered(): pl.pallas_call(local_kernel, out_shape=(jax.ShapeDtypeStruct((2, span, wi...  2.51 us
    unnamed x8, local copies, waits for them, and re-layouts  1.71 us
  transfers between devices with their start and end apart: 14, of which 6 were waited for; matrix products, arithmetic and copies ran while one was open for 0% of the time, Pallas kernels for 0%

profile of v1, /device:TPU:0, one launch (start us, length us, event | category | flops | bytes accessed | tf_op | source)
XLA Modules:
  0.0 30.9 jit_solution(17811037323713084950)
XLA Ops:
  0.6 0.0 copy-start
  0.6 0.9 %copy-done = bf16[2,128,512]{2,1,0:T(8,128)(2,1)S(1)} copy-done((bf16[2,128,512]{2,1,0:T(8,128)(2,1)S(1)}, bf16[2,128,512]{2,1,0:T(8,128)(2,1)}, u32[]{:S(2)}) %copy-start) | copy-done | bytes 262168
  1.6 0.0 copy-start.2
  1.6 0.8 %copy-done.2 = f32[128,64]{0,1:T(8,128)S(1)} copy-done((f32[128,64]{0,1:T(8,128)S(1)}, f32[128,64]{0,1:T(8,128)}, u32[]{:S(2)}) %copy-start.2) | copy-done | bytes 32792
  2.3 0.0 copy-start.1
  2.3 0.2 shard_map.50
  2.6 4.1 %collective-permute-start.2 = (bf16[4,128,128]{2,1,0:T(8,128)(2,1)S(1)}, bf16[4,128,128]{2,1,0:T(8,128)(2,1)S(1)}, u32[]{:S(2)}, u32[]{:S(2)}) collective-permute-start(bf16[4,128,128]{2,1,0:T(8,128)(2,1)S(1)} %get-tuple-element.9), channel_id=1, source_target_pairs={{0,16},{8,24},{16,0},{24,8},{1,17},{9,25},{17,1},{25,9},{2,18},{10... | collective-permute-start | bytes 393224 | tf_op jit(solution)/shard_map/ppermute | solution.py:253
  6.7 1.3 %collective-permute-start.6 = (bf16[2,128,128]{2,1,0:T(8,128)(2,1)S(1)}, bf16[2,128,128]{2,1,0:T(8,128)(2,1)S(1)}, u32[]{:S(2)}, u32[]{:S(2)}) collective-permute-start(bf16[2,128,128]{2,1,0:T(8,128)(2,1)S(1)} %get-tuple-element.11), channel_id=1, source_target_pairs={{0,24},{8,16},{16,8},{24,0},{1,25},{9,17},{17,9},{25,1},{2,26},{10... | collective-permute-start | bytes 196616 | tf_op jit(solution)/shard_map/ppermute | solution.py:253
  8.1 1.7 %collective-permute-start.5 = (bf16[128,128]{1,0:T(8,128)(2,1)S(1)}, bf16[128,128]{1,0:T(8,128)(2,1)S(1)}, u32[]{:S(2)}, u32[]{:S(2)}) collective-permute-start(bf16[128,128]{1,0:T(8,128)(2,1)S(1)} %get-tuple-element.10.own), channel_id=1, source_target_pairs={{0,16},{8,24},{16,0},{24,8},{1,17},{9,25},{17,1},{25,9},{2,18},{10... | collective-permute-start | bytes 98312 | tf_op jit(solution)/shard_map/ppermute | solution.py:253
  9.8 1.3 %collective-permute-start.4 = (bf16[128,128]{1,0:T(8,128)(2,1)S(1)}, bf16[128,128]{1,0:T(8,128)(2,1)S(1)}, u32[]{:S(2)}, u32[]{:S(2)}) collective-permute-start(bf16[128,128]{1,0:T(8,128)(2,1)S(1)} %get-tuple-element.10.own), channel_id=1, source_target_pairs={{0,8},{8,0},{16,24},{24,16},{1,9},{9,1},{17,25},{25,17},{2,10},{10... | collective-permute-start | bytes 98312 | tf_op jit(solution)/shard_map/ppermute | solution.py:253
  11.1 6.1 %collective-permute-done.5.second = bf16[128,128]{1,0:T(8,128)(2,1)S(1)} collective-permute-done((bf16[128,128]{1,0:T(8,128)(2,1)S(1)}, bf16[128,128]{1,0:T(8,128)(2,1)S(1)}, u32[]{:S(2)}, u32[]{:S(2)}) %collective-permute-start.5) | collective-permute-done | bytes 32800 | tf_op jit(solution)/shard_map/ppermute | solution.py:253
  17.2 0.0 collective-permute-done.4.first
  17.2 0.0 collective-permute-done.6.last
  17.2 0.1 shard_map.51
  17.4 0.1 collective-permute-start.7
  17.5 0.8 %collective-permute-start = (bf16[4,128,128]{2,1,0:T(8,128)(2,1)S(1)}, bf16[4,128,128]{2,1,0:T(8,128)(2,1)S(1)}, u32[]{:S(2)}, u32[]{:S(2)}) collective-permute-start(bf16[4,128,128]{2,1,0:T(8,128)(2,1)S(1)} %get-tuple-element.9), channel_id=1, source_target_pairs={{0,8},{8,0},{16,24},{24,16},{1,9},{9,1},{17,25},{25,17},{2,10},{10... | collective-permute-start | bytes 393224 | tf_op jit(solution)/shard_map/ppermute | solution.py:253
  18.2 1.5 %collective-permute-start.8 = (bf16[416,128]{1,0:T(8,128)(2,1)S(1)}, bf16[416,128]{1,0:T(8,128)(2,1)S(1)}, u32[]{:S(2)}, u32[]{:S(2)}) collective-permute-start(bf16[416,128]{1,0:T(8,128)(2,1)S(1)} %get-tuple-element.13), channel_id=1, source_target_pairs={{0,2},{1,3},{2,0},{3,1},{4,6},{5,7},{6,4},{7,5},{8,10},{9,11},{10,... | collective-permute-start | bytes 319496 | tf_op jit(solution)/shard_map/ppermute | solution.py:253
  19.7 0.0 copy-start.3
  19.7 1.5 %collective-permute-start.10 = (bf16[416,128]{1,0:T(8,128)(2,1)S(1)}, bf16[416,128]{1,0:T(8,128)(2,1)S(1)}, u32[]{:S(2)}, u32[]{:S(2)}) collective-permute-start(bf16[416,128]{1,0:T(8,128)(2,1)S(1)} %get-tuple-element.14), channel_id=1, source_target_pairs={{0,4},{1,5},{2,6},{3,7},{4,0},{5,1},{6,2},{7,3},{8,12},{9,13},{10,... | collective-permute-start | bytes 319496 | tf_op jit(solution)/shard_map/ppermute | solution.py:253
  21.3 0.0 collective-permute-done.2.refs_2_
  21.3 0.5 %collective-permute-start.12 = (bf16[416,128]{1,0:T(8,128)(2,1)S(1)}, bf16[416,128]{1,0:T(8,128)(2,1)S(1)}, u32[]{:S(2)}, u32[]{:S(2)}) collective-permute-start(bf16[416,128]{1,0:T(8,128)(2,1)S(1)} %get-tuple-element.15), channel_id=1, source_target_pairs={{0,6},{1,7},{2,4},{3,5},{4,2},{5,3},{6,0},{7,1},{8,14},{9,15},{10,... | collective-permute-start | bytes 319496 | tf_op jit(solution)/shard_map/ppermute | solution.py:253
  21.7 1.6 %collective-permute-done.refs_0_ = bf16[4,128,128]{2,1,0:T(8,128)(2,1)S(1)} collective-permute-done((bf16[4,128,128]{2,1,0:T(8,128)(2,1)S(1)}, bf16[4,128,128]{2,1,0:T(8,128)(2,1)S(1)}, u32[]{:S(2)}, u32[]{:S(2)}) %collective-permute-start) | collective-permute-done | bytes 131104 | tf_op jit(solution)/shard_map/ppermute | solution.py:253
  23.4 0.0 collective-permute-start.3
  23.4 0.0 collective-permute-done.8.refs_6_
  23.4 0.5 %collective-permute-start.1 = (bf16[4,128,128]{2,1,0:T(8,128)(2,1)S(1)}, bf16[4,128,128]{2,1,0:T(8,128)(2,1)S(1)}, u32[]{:S(2)}, u32[]{:S(2)}) collective-permute-start(bf16[4,128,128]{2,1,0:T(8,128)(2,1)S(1)} %collective-permute-done.refs_0_), channel_id=1, source_target_pairs={{0,1},{1,0},{2,3},{3,2},{4,5},{5,4},{6,7},{7,6},{8,9},{9,8},{10,11... | collective-permute-start | bytes 393224 | tf_op jit(solution)/shard_map/ppermute | solution.py:253
  23.9 1.9 %collective-permute-done.10.refs_8_ = bf16[416,128]{1,0:T(8,128)(2,1)S(1)} collective-permute-done((bf16[416,128]{1,0:T(8,128)(2,1)S(1)}, bf16[416,128]{1,0:T(8,128)(2,1)S(1)}, u32[]{:S(2)}, u32[]{:S(2)}) %collective-permute-start.10) | collective-permute-done | bytes 106528 | tf_op jit(solution)/shard_map/ppermute | solution.py:253
  25.8 0.0 collective-permute-start.9
  25.8 1.1 %collective-permute-done.12.refs_10_ = bf16[416,128]{1,0:T(8,128)(2,1)S(1)} collective-permute-done((bf16[416,128]{1,0:T(8,128)(2,1)S(1)}, bf16[416,128]{1,0:T(8,128)(2,1)S(1)}, u32[]{:S(2)}, u32[]{:S(2)}) %collective-permute-start.12) | collective-permute-done | bytes 106528 | tf_op jit(solution)/shard_map/ppermute | solution.py:253
  26.9 0.0 collective-permute-start.11
  26.9 0.0 collective-permute-done.7.refs_5_
  26.9 0.5 %collective-permute-start.13 = (bf16[416,128]{1,0:T(8,128)(2,1)S(1)}, bf16[416,128]{1,0:T(8,128)(2,1)S(1)}, u32[]{:S(2)}, u32[]{:S(2)}) collective-permute-start(bf16[416,128]{1,0:T(8,128)(2,1)S(1)} %collective-permute-done.12.refs_10_), channel_id=1, source_target_pairs={{0,1},{1,0},{2,3},{3,2},{4,5},{5,4},{6,7},{7,6},{8,9},{9,8},{10,11... | collective-permute-start | bytes 319496 | tf_op jit(solution)/shard_map/ppermute | solution.py:253
  27.4 0.0 collective-permute-done.3.refs_3_
  27.4 0.0 collective-permute-done.1.refs_1_
  27.4 0.0 collective-permute-done.9.refs_7_
  27.4 0.8 %collective-permute-done.11.refs_9_ = bf16[416,128]{1,0:T(8,128)(2,1)S(1)} collective-permute-done((bf16[416,128]{1,0:T(8,128)(2,1)S(1)}, bf16[416,128]{1,0:T(8,128)(2,1)S(1)}, u32[]{:S(2)}, u32[]{:S(2)}) %collective-permute-start.11) | collective-permute-done | bytes 106528 | tf_op jit(solution)/shard_map/ppermute | solution.py:253
  28.2 0.2 collective-permute-done.13.refs_11_
  28.3 0.0 copy-done.1
  28.3 0.0 copy-done.3
  28.3 2.5 %shard_map.52 = (f32[2,16,512]{2,1,0:T(8,128)}, f32[2,64,512]{2,1,0:T(8,128)}) custom-call(s32[2,4]{1,0:T(2,128)S(1)} %copy-done.3, bf16[2,128,512]{2,1,0:T(8,128)(2,1)S(1)} %copy-done.1, bf16[4,128,128]{2,1,0:T(8,128)(2,1)S(1)} %collective-permute-done.refs_0_, bf16[4,128,128]{2,1,0:T(8,128)(2,1)S(1)} %collective-permute-done.1.refs_1_, ...), custom_call_target="tpu_custom_call" | custom-call | tf_op jit(solution)/shard_map/pallas_call | solution.py:285
Async XLA Ops:
  0.6 1.0 %copy-start = (bf16[2,128,512]{2,1,0:T(8,128)(2,1)S(1)}, bf16[2,128,512]{2,1,0:T(8,128)(2,1)}, u32[]{:S(2)}) copy-start(bf16[2,128,512]{2,1,0:T(8,128)(2,1)} %panels_ref.1) | copy-start | bytes 786436
  1.6 0.8 %copy-start.2 = (f32[128,64]{0,1:T(8,128)S(1)}, f32[128,64]{0,1:T(8,128)}, u32[]{:S(2)}) copy-start(f32[128,64]{0,1:T(8,128)} %param.3) | copy-start | bytes 98308
  2.3 26.0 %copy-start.1 = (bf16[2,128,512]{2,1,0:T(8,128)(2,1)S(1)}, bf16[2,128,512]{2,1,0:T(8,128)(2,1)}, u32[]{:S(2)}) copy-start(bf16[2,128,512]{2,1,0:T(8,128)(2,1)} %panels_ref.1) | copy-start | bytes 786436
  2.6 18.7 %collective-permute-start.2 = (bf16[4,128,128]{2,1,0:T(8,128)(2,1)S(1)}, bf16[4,128,128]{2,1,0:T(8,128)(2,1)S(1)}, u32[]{:S(2)}, u32[]{:S(2)}) collective-permute-start(bf16[4,128,128]{2,1,0:T(8,128)(2,1)S(1)} %get-tuple-element.9), channel_id=1, source_target_pairs={{0,16},{8,24},{16,0},{24,8},{1,17},{9,25},{17,1},{25,9},{2,18},{10... | collective-permute-start | bytes 393224 | tf_op jit(solution)/shard_map/ppermute | solution.py:253
  6.7 10.5 %collective-permute-start.6 = (bf16[2,128,128]{2,1,0:T(8,128)(2,1)S(1)}, bf16[2,128,128]{2,1,0:T(8,128)(2,1)S(1)}, u32[]{:S(2)}, u32[]{:S(2)}) collective-permute-start(bf16[2,128,128]{2,1,0:T(8,128)(2,1)S(1)} %get-tuple-element.11), channel_id=1, source_target_pairs={{0,24},{8,16},{16,8},{24,0},{1,25},{9,17},{17,9},{25,1},{2,26},{10... | collective-permute-start | bytes 196616 | tf_op jit(solution)/shard_map/ppermute | solution.py:253
  8.1 9.2 %collective-permute-start.5 = (bf16[128,128]{1,0:T(8,128)(2,1)S(1)}, bf16[128,128]{1,0:T(8,128)(2,1)S(1)}, u32[]{:S(2)}, u32[]{:S(2)}) collective-permute-start(bf16[128,128]{1,0:T(8,128)(2,1)S(1)} %get-tuple-element.10.own), channel_id=1, source_target_pairs={{0,16},{8,24},{16,0},{24,8},{1,17},{9,25},{17,1},{25,9},{2,18},{10... | collective-permute-start | bytes 98312 | tf_op jit(solution)/shard_map/ppermute | solution.py:253
  9.8 7.5 %collective-permute-start.4 = (bf16[128,128]{1,0:T(8,128)(2,1)S(1)}, bf16[128,128]{1,0:T(8,128)(2,1)S(1)}, u32[]{:S(2)}, u32[]{:S(2)}) collective-permute-start(bf16[128,128]{1,0:T(8,128)(2,1)S(1)} %get-tuple-element.10.own), channel_id=1, source_target_pairs={{0,8},{8,0},{16,24},{24,16},{1,9},{9,1},{17,25},{25,17},{2,10},{10... | collective-permute-start | bytes 98312 | tf_op jit(solution)/shard_map/ppermute | solution.py:253
  17.4 9.5 %collective-permute-start.7 = (bf16[672,128]{1,0:T(8,128)(2,1)S(1)}, bf16[672,128]{1,0:T(8,128)(2,1)S(1)}, u32[]{:S(2)}, u32[]{:S(2)}) collective-permute-start(bf16[672,128]{1,0:T(8,128)(2,1)S(1)} %get-tuple-element.12.refs_4_), channel_id=1, source_target_pairs={{0,1},{1,0},{2,3},{3,2},{4,5},{5,4},{6,7},{7,6},{8,9},{9,8},{10,11... | collective-permute-start | bytes 516104 | tf_op jit(solution)/shard_map/ppermute | solution.py:253
  17.5 5.9 %collective-permute-start = (bf16[4,128,128]{2,1,0:T(8,128)(2,1)S(1)}, bf16[4,128,128]{2,1,0:T(8,128)(2,1)S(1)}, u32[]{:S(2)}, u32[]{:S(2)}) collective-permute-start(bf16[4,128,128]{2,1,0:T(8,128)(2,1)S(1)} %get-tuple-element.9), channel_id=1, source_target_pairs={{0,8},{8,0},{16,24},{24,16},{1,9},{9,1},{17,25},{25,17},{2,10},{10... | collective-permute-start | bytes 393224 | tf_op jit(solution)/shard_map/ppermute | solution.py:253
  18.2 5.1 %collective-permute-start.8 = (bf16[416,128]{1,0:T(8,128)(2,1)S(1)}, bf16[416,128]{1,0:T(8,128)(2,1)S(1)}, u32[]{:S(2)}, u32[]{:S(2)}) collective-permute-start(bf16[416,128]{1,0:T(8,128)(2,1)S(1)} %get-tuple-element.13), channel_id=1, source_target_pairs={{0,2},{1,3},{2,0},{3,1},{4,6},{5,7},{6,4},{7,5},{8,10},{9,11},{10,... | collective-permute-start | bytes 319496 | tf_op jit(solution)/shard_map/ppermute | solution.py:253
  19.7 8.6 %copy-start.3 = (s32[2,4]{1,0:T(2,128)S(1)}, s32[2,4]{1,0:T(2,128)}, u32[]{:S(2)}) copy-start(s32[2,4]{1,0:T(2,128)} %pattern_ref.1) | copy-start | bytes 100
  19.7 6.1 %collective-permute-start.10 = (bf16[416,128]{1,0:T(8,128)(2,1)S(1)}, bf16[416,128]{1,0:T(8,128)(2,1)S(1)}, u32[]{:S(2)}, u32[]{:S(2)}) collective-permute-start(bf16[416,128]{1,0:T(8,128)(2,1)S(1)} %get-tuple-element.14), channel_id=1, source_target_pairs={{0,4},{1,5},{2,6},{3,7},{4,0},{5,1},{6,2},{7,3},{8,12},{9,13},{10,... | collective-permute-start | bytes 319496 | tf_op jit(solution)/shard_map/ppermute | solution.py:253
  21.3 5.6 %collective-permute-start.12 = (bf16[416,128]{1,0:T(8,128)(2,1)S(1)}, bf16[416,128]{1,0:T(8,128)(2,1)S(1)}, u32[]{:S(2)}, u32[]{:S(2)}) collective-permute-start(bf16[416,128]{1,0:T(8,128)(2,1)S(1)} %get-tuple-element.15), channel_id=1, source_target_pairs={{0,6},{1,7},{2,4},{3,5},{4,2},{5,3},{6,0},{7,1},{8,14},{9,15},{10,... | collective-permute-start | bytes 319496 | tf_op jit(solution)/shard_map/ppermute | solution.py:253
  23.4 4.0 %collective-permute-start.3 = (bf16[4,128,128]{2,1,0:T(8,128)(2,1)S(1)}, bf16[4,128,128]{2,1,0:T(8,128)(2,1)S(1)}, u32[]{:S(2)}, u32[]{:S(2)}) collective-permute-start(bf16[4,128,128]{2,1,0:T(8,128)(2,1)S(1)} %collective-permute-done.2.refs_2_), channel_id=1, source_target_pairs={{0,1},{1,0},{2,3},{3,2},{4,5},{5,4},{6,7},{7,6},{8,9},{9,8},{10,11... | collective-permute-start | bytes 393224 | tf_op jit(solution)/shard_map/ppermute | solution.py:253
  23.4 4.0 %collective-permute-start.1 = (bf16[4,128,128]{2,1,0:T(8,128)(2,1)S(1)}, bf16[4,128,128]{2,1,0:T(8,128)(2,1)S(1)}, u32[]{:S(2)}, u32[]{:S(2)}) collective-permute-start(bf16[4,128,128]{2,1,0:T(8,128)(2,1)S(1)} %collective-permute-done.refs_0_), channel_id=1, source_target_pairs={{0,1},{1,0},{2,3},{3,2},{4,5},{5,4},{6,7},{7,6},{8,9},{9,8},{10,11... | collective-permute-start | bytes 393224 | tf_op jit(solution)/shard_map/ppermute | solution.py:253
  25.8 1.6 %collective-permute-start.9 = (bf16[416,128]{1,0:T(8,128)(2,1)S(1)}, bf16[416,128]{1,0:T(8,128)(2,1)S(1)}, u32[]{:S(2)}, u32[]{:S(2)}) collective-permute-start(bf16[416,128]{1,0:T(8,128)(2,1)S(1)} %collective-permute-done.8.refs_6_), channel_id=1, source_target_pairs={{0,1},{1,0},{2,3},{3,2},{4,5},{5,4},{6,7},{7,6},{8,9},{9,8},{10,11... | collective-permute-start | bytes 319496 | tf_op jit(solution)/shard_map/ppermute | solution.py:253
  26.9 1.3 %collective-permute-start.11 = (bf16[416,128]{1,0:T(8,128)(2,1)S(1)}, bf16[416,128]{1,0:T(8,128)(2,1)S(1)}, u32[]{:S(2)}, u32[]{:S(2)}) collective-permute-start(bf16[416,128]{1,0:T(8,128)(2,1)S(1)} %collective-permute-done.10.refs_8_), channel_id=1, source_target_pairs={{0,1},{1,0},{2,3},{3,2},{4,5},{5,4},{6,7},{7,6},{8,9},{9,8},{10,11... | collective-permute-start | bytes 319496 | tf_op jit(solution)/shard_map/ppermute | solution.py:253
  26.9 1.5 %collective-permute-start.13 = (bf16[416,128]{1,0:T(8,128)(2,1)S(1)}, bf16[416,128]{1,0:T(8,128)(2,1)S(1)}, u32[]{:S(2)}, u32[]{:S(2)}) collective-permute-start(bf16[416,128]{1,0:T(8,128)(2,1)S(1)} %collective-permute-done.12.refs_10_), channel_id=1, source_target_pairs={{0,1},{1,0},{2,3},{3,2},{4,5},{5,4},{6,7},{7,6},{8,9},{9,8},{10,11... | collective-permute-start | bytes 319496 | tf_op jit(solution)/shard_map/ppermute | solution.py:253
